TPU v7x, 128 devices: a whole 4x4x4 slice. The times are simulated.
128 devices in a mesh: row: 16 (over x_hi, y, core), col: 8 (over z, x_lo).
Axes of the slice: x: 4 (x_hi: 2, x_lo: 2; x = x_hi * 2 + x_lo), y: 4, z: 4, core: 2. Of those that a mesh axis runs over, the one named last changes fastest.
Arguments:
- values: float32 [8192, 8192], P('row', 'col'), may hold values from 0 to 10, as said below
- pattern: int32 [64, 64], replicated, may hold values from 0 to 1, as said below
- pruning: int32 [64, 64], replicated, may hold values from 0 to 1, as said below
- owners: int32 [64], replicated, may hold values from 0 to 63, as said below
Outputs:
- expanded: float32 [8192, 8192], P('row', 'col')
Inputs may be any that keep to these rules, and one draw needn't show every extreme that they name: `values`: positive scores. `pattern`: every diagonal block is present. `pruning`: every diagonal block is kept. `owners`: A permutation of the 64 column blocks. Of the 8 column blocks of one index of col, at most 2 are stored at the column blocks of any one index of col, and exactly 2 at those of some index.
All inputs are finite; a program needn't handle non-finite values.
Results may differ from a plain program's by a relative error of at most 0.00065.
Values may be sent and summed in bfloat16 or wider, within the bound.
No kernel may reach another device: no remote copies, remote signals or barrier semaphores. Data moves between devices by JAX's collectives and lax.ppermute only.
A program may use at most 128 MiB of HBM per device.

v0:
```python
import jax
import jax.numpy as jnp
from jax import lax
from jax.sharding import PartitionSpec as P

BLK = 128


def expand_mask(tile, mask, blk):
    rows_in, cols_in = tile.shape
    shaped = tile.reshape(rows_in // blk, blk, cols_in // blk, blk)
    return (shaped * mask.astype(tile.dtype)[:, None, :, None]).reshape(rows_in, cols_in)


def ranks_of(destination):
    width = destination.shape[-1]
    earlier = jnp.arange(width)[:, None] < jnp.arange(width)[None, :]
    same_dest = destination[..., :, None] == destination[..., None, :]
    return jnp.sum(jnp.where(same_dest & earlier, 1, 0), axis=-2).astype(jnp.int32)


def pack_blocks(tile, owners, me_col, ncols, capacity, blk):
    rows_in, cols_in = tile.shape
    width = cols_in // blk
    my_owners = lax.dynamic_slice(owners, (me_col * width,), (width,))
    destination = my_owners // width
    rank = ranks_of(destination)
    slot_ids = jnp.arange(ncols * capacity)
    selector = (
        (destination[None, :] == (slot_ids // capacity)[:, None])
        & (rank[None, :] == (slot_ids % capacity)[:, None])
    ).astype(tile.dtype)
    column_blocks = tile.reshape(rows_in, width, blk)
    outgoing = jnp.einsum(
        "pk,rkb->prb",
        selector,
        column_blocks,
        preferred_element_type=jnp.float32,
        precision=lax.Precision.HIGHEST,
    )
    return outgoing


def unpack_blocks(arrived, owners, me_col, ncols, capacity):
    slot_count, rows_in, blk = arrived.shape
    width = owners.shape[0] // ncols
    table = owners.reshape(ncols, width)
    rank = ranks_of(table // width)
    wanted = me_col * width + jnp.arange(width)
    matches = table[None, :, :] == wanted[:, None, None]
    which_slot = rank[:, :, None] == jnp.arange(capacity)[None, None, :]
    selector = jnp.sum(jnp.where(matches[:, :, :, None] & which_slot[None], 1, 0), axis=2)
    selector = selector.reshape(width, ncols * capacity).astype(arrived.dtype)
    placed = jnp.einsum(
        "sp,prb->rsb",
        selector,
        arrived,
        preferred_element_type=jnp.float32,
        precision=lax.Precision.HIGHEST,
    )
    return placed.reshape(rows_in, width * blk)


def body(values, pattern, pruning, owners):
    rows_dev, cols_dev = values.shape
    blk = BLK
    row_blocks = rows_dev // blk
    col_blocks = cols_dev // blk
    ncols = lax.axis_size("col")
    capacity = max(2, (col_blocks + ncols - 1) // ncols)
    me_row = lax.axis_index("row")
    me_col = lax.axis_index("col")
    local_pattern = lax.dynamic_slice(
        pattern, (me_row * row_blocks, me_col * col_blocks), (row_blocks, col_blocks)
    )
    masked = expand_mask(values, local_pattern, blk)
    colsum_in = lax.psum(jnp.sum(masked, axis=0), "row")
    stochastic = (masked / colsum_in[None, :]).astype(jnp.bfloat16)
    row_panel = lax.all_gather(stochastic, "col", axis=1, tiled=True)
    nodes = row_panel.shape[1]
    pruning_rows = lax.dynamic_slice(
        pruning, (me_row * row_blocks, 0), (row_blocks, pruning.shape[1])
    )
    kept_mask = lax.dynamic_slice_in_dim(pruning_rows, me_col * col_blocks, col_blocks, 1)
    square = jnp.dot(
        row_panel,
        lax.all_gather(stochastic, "row", axis=0, tiled=True),
        preferred_element_type=jnp.float32,
    )
    inflated = expand_mask(square * square, kept_mask, blk)
    colsum_out = lax.psum(jnp.sum(inflated, axis=0), "row")
    normalized = jnp.float32(nodes) * inflated / colsum_out[None, :]
    arrived_out = lax.all_to_all(
        pack_blocks(normalized, owners, me_col, ncols, capacity, blk),
        "col",
        split_axis=0,
        concat_axis=0,
        tiled=True,
    )
    result = unpack_blocks(arrived_out, owners, me_col, ncols, capacity)
    return result


def solution(mesh):
    return jax.shard_map(
        body,
        mesh=mesh,
        in_specs=(P("row", "col"), P(), P(), P()),
        out_specs=P("row", "col"),
        check_vma=False,
    )
```

profile of v0, /device:TPU:0, one launch (start us, length us, event | category | flops | bytes accessed | tf_op | source)
XLA Modules:
  0.0 452.6 jit_solution(7957865634004855820)
XLA Ops:
  6.5 0.9 dynamic-slice_convert_fusion.1
  7.4 0.2 mul.43
  7.7 0.5 copy-done
  8.1 0.7 fusion.2
  8.8 38.2 %psum.14 = f32[1024]{0:T(1024)S(1)} all-reduce(f32[1024]{0:T(1024)S(1)} %fusion.2), channel_id=1, replica_groups=mesh['row'=16,'col'=8] {'row'}, use_global_device_ids=true, to_apply=%region_2.0 | all-reduce | flops 1024 | bytes 8192 | tf_op jit(solution)/shard_map/psum | solution.py:77
  47.0 3.2 divide_convert_fusion
  50.3 0.7 all-gather.5.cloned.1.call-update
  51.1 0.8 dynamic-slice_convert_fusion
  51.9 0.1 select_reduce_fusion.2
  52.0 164.6 %all-gather.3.cloned.1.call-done = bf16[512,8192]{1,0:T(8,128)(2,1)} async-done(((bf16[512,1024]{1,0:T(8,128)(2,1)}), bf16[512,8192]{1,0:T(8,128)(2,1)}) %all-gather.3.cloned.1.call-update) | async-done | bytes 8388624 | tf_op jit(solution)/shard_map/all_gather | solution.py:79
  216.6 112.1 %all-gather.5.cloned.1.call-done = bf16[8192,1024]{1,0:T(8,128)(2,1)} async-done(((bf16[512,1024]{1,0:T(8,128)(2,1)}), bf16[8192,1024]{1,0:T(8,128)(2,1)}) %all-gather.5.cloned.1.call-update) | async-done | bytes 16777232 | tf_op jit(solution)/shard_map/all_gather | solution.py:87
  328.7 0.2 mul.47
  328.9 14.8 %fusion.14 = (f32[1024]{0:T(1024)S(1)}, f32[512,1024]{1,0:T(8,128)S(1)}) fusion(f32[64,8,8,128]{3,2,1,0:T(8,128)S(1)} %bitcast.34, bf16[512,8192]{1,0:T(8,128)(2,1)} %all-gather.3.cloned.1.call-done, bf16[8192,1024]{1,0:T(8,128)(2,1)} %all-gather.5.cloned.1.call-done), kind=kOutput, calls=%fused_computation.43 | convolution fusion | flops 8591506432 | bytes 29364224 | tf_op jit(solution)/shard_map/dot_general | solution.py:85
  343.7 33.8 %psum.15 = f32[1024]{0:T(1024)S(1)} all-reduce(f32[1024]{0:T(1024)S(1)} %get-tuple-element.5), channel_id=1, replica_groups=mesh['row'=16,'col'=8] {'row'}, use_global_device_ids=true, to_apply=%region_4.5 | all-reduce | flops 1024 | bytes 8192 | tf_op jit(solution)/shard_map/psum | solution.py:91
  377.6 0.3 divide_bitcast_fusion
  377.8 0.5 copy.21
  378.3 1.9 fusion.5
  380.2 3.3 copy.12
  383.5 5.3 %all-to-all-start = ((f32[16,512,128]{2,1,0:T(8,128)}), f32[16,512,128]{2,1,0:T(8,128)}, u32[]{:S(2)}, u32[]{:S(2)}) async-start(f32[16,512,128]{2,1,0:T(8,128)} %copy.12), calls=%async_computation | async-start | bytes 8388608 | tf_op jit(solution)/shard_map/all_to_all | solution.py:93
  388.9 0.1 select_reduce_fusion.1
  389.1 0.4 select_reduce_fusion
  389.6 47.6 %all-to-all-done = f32[16,512,128]{2,1,0:T(8,128)} async-done(((f32[16,512,128]{2,1,0:T(8,128)}), f32[16,512,128]{2,1,0:T(8,128)}, u32[]{:S(2)}, u32[]{:S(2)}) %all-to-all-start) | async-done | bytes 4194336 | tf_op jit(solution)/shard_map/all_to_all | solution.py:93
  437.1 6.8 %fusion = f32[512,128,8]{1,2,0:T(8,128)S(1)} fusion(f32[8,16,1]{0,1,2:T(8,128)S(1)} %bitcast.35, f32[16,512,128]{2,1,0:T(8,128)} %all-to-all-done), kind=kOutput, calls=%fused_computation | convolution fusion | flops 100663296 | bytes 6291968 | tf_op jit(solution)/shard_map/sp,prb->rsb/dot_general | solution.py:54
  444.0 1.8 copy.33
  (16 shorter events, 0.4 us)
Async XLA Ops:
  6.5 210.1 %all-gather.3.cloned.1.call-start = ((), (), s32[]{:S(2)}) async-start(), calls=%async_computation.1 | async-start | bytes 9437184 | tf_op jit(solution)/shard_map/all_gather | solution.py:79
  6.5 1.6 copy-start
  50.2 0.8 copy-start.1
  50.3 278.4 %all-gather.5.cloned.1.call-start = ((), (), s32[]{:S(2)}) async-start(), calls=%async_computation.2 | async-start | bytes 17825792 | tf_op jit(solution)/shard_map/all_gather | solution.py:87
  383.5 53.7 %all-to-all-start = ((f32[16,512,128]{2,1,0:T(8,128)}), f32[16,512,128]{2,1,0:T(8,128)}, u32[]{:S(2)}, u32[]{:S(2)}) async-start(f32[16,512,128]{2,1,0:T(8,128)} %copy.12), calls=%async_computation | async-start | bytes 8388608 | tf_op jit(solution)/shard_map/all_to_all | solution.py:93
Sparse Core Ops, SparseCore 0:
  50.4 166.1 all-gather.2
  219.0 109.6 all-gather.4
where the time goes:
time: 453 us
  waiting for transfers between devices  325 us (72%)
  blocking collectives  72 us (16%)
  matrix products  23.5 us (5%)
  between operations  13.5 us (3%)
  other arithmetic  6.6 us (1%)
  local copies, waits for them, and re-layouts  6.55 us (1%)
  starting transfers between devices  5.38 us (1%)
    all_gather x1, waiting for transfers between devices, body(): row_panel = lax.all_gather(stochastic, 'col', axis=1, tiled=True)  165 us
    all_gather x1, waiting for transfers between devices, body(): lax.all_gather(stochastic, 'row', axis=0, tiled=True)  112 us
    all_to_all x1, waiting for transfers between devices, body(): lax.all_to_all(pack_blocks(normalized, owners, me_col, ncols, capacity, b...  47.6 us
    psum x1, blocking collectives, body(): colsum_in = lax.psum(jnp.sum(masked, axis=0), 'row')  38.2 us
    psum x1, blocking collectives, body(): colsum_out = lax.psum(jnp.sum(inflated, axis=0), 'row')  33.8 us
    dot_general x1, matrix products, body(): jnp.dot(row_panel, lax.all_gather(stochastic, 'row', axis=0, tiled=True),...  14.8 us
  transfers between devices with their start and end apart: 3, of which 3 were waited for; matrix products, arithmetic and copies ran while one was open for 0% of the time, Pallas kernels for 0%

commit v1 on v0

--- a/solution.py
+++ b/solution.py
@@ -74,7 +74,7 @@
         pattern, (me_row * row_blocks, me_col * col_blocks), (row_blocks, col_blocks)
     )
     masked = expand_mask(values, local_pattern, blk)
-    colsum_in = lax.psum(jnp.sum(masked, axis=0), "row")
+    colsum_in = jnp.sum(lax.all_gather(jnp.sum(masked, axis=0), "row"), axis=0)
     stochastic = (masked / colsum_in[None, :]).astype(jnp.bfloat16)
     row_panel = lax.all_gather(stochastic, "col", axis=1, tiled=True)
     nodes = row_panel.shape[1]

time: 453 us -> 439 us (0.969)
  blocking collectives: 72 us -> 58.5 us
    psum x1 -> x0, blocking collectives: 38.2 us -> none  [body(): colsum_in = lax.psum(jnp.sum(masked, axis=0), 'row')]
    all_gather x0 -> x1, blocking collectives: none -> 24.7 us  [body(): colsum_in = jnp.sum(lax.all_gather(jnp.sum(masked, axis=0), 'row'), axis=0)]
where the time goes in v1:
time: 439 us
  waiting for transfers between devices  325 us (74%)
  blocking collectives  58.5 us (13%)
  matrix products  23.5 us (5%)
  between operations  13.5 us (3%)
  other arithmetic  6.62 us (2%)
  local copies, waits for them, and re-layouts  6.57 us (1%)
  starting transfers between devices  5.38 us (1%)
    all_gather x1, waiting for transfers between devices, body(): row_panel = lax.all_gather(stochastic, 'col', axis=1, tiled=True)  165 us
    all_gather x1, waiting for transfers between devices, body(): lax.all_gather(stochastic, 'row', axis=0, tiled=True)  112 us
    all_to_all x1, waiting for transfers between devices, body(): lax.all_to_all(pack_blocks(normalized, owners, me_col, ncols, capacity, b...  47.6 us
    psum x1, blocking collectives, body(): colsum_out = lax.psum(jnp.sum(inflated, axis=0), 'row')  33.8 us
    all_gather x1, blocking collectives, body(): colsum_in = jnp.sum(lax.all_gather(jnp.sum(masked, axis=0), 'row'), axis=0)  24.7 us
    dot_general x1, matrix products, body(): jnp.dot(row_panel, lax.all_gather(stochastic, 'row', axis=0, tiled=True),...  14.8 us
  transfers between devices with their start and end apart: 3, of which 3 were waited for; matrix products, arithmetic and copies ran while one was open for 0% of the time, Pallas kernels for 0%

profile of v1, /device:TPU:0, one launch (start us, length us, event | category | flops | bytes accessed | tf_op | source)
XLA Modules:
  0.0 439.1 jit_solution(11374440091912384503)
XLA Ops:
  6.5 0.9 dynamic-slice_convert_fusion.1
  7.4 0.2 mul.43
  7.7 0.5 copy-done
  8.1 0.7 fusion.2
  8.8 24.7 %all-gather = f32[16384]{0:T(1024)S(1)} all-gather(f32[1024]{0:T(1024)S(1)} %fusion.2), channel_id=2, replica_groups=mesh['row'=16,'col'=8] {'row'}, dimensions={0}, use_global_device_ids=true | all-gather | bytes 69632 | tf_op jit(solution)/shard_map/all_gather | solution.py:77
  33.6 3.2 divide_convert_fusion
  36.9 0.7 all-gather.6.cloned.1.call-update
  37.7 0.8 dynamic-slice_convert_fusion
  38.4 0.1 select_reduce_fusion.2
  38.5 164.6 %all-gather.4.cloned.1.call-done = bf16[512,8192]{1,0:T(8,128)(2,1)} async-done(((bf16[512,1024]{1,0:T(8,128)(2,1)}), bf16[512,8192]{1,0:T(8,128)(2,1)}) %all-gather.4.cloned.1.call-update) | async-done | bytes 8388624 | tf_op jit(solution)/shard_map/all_gather | solution.py:79
  203.1 112.1 %all-gather.6.cloned.1.call-done = bf16[8192,1024]{1,0:T(8,128)(2,1)} async-done(((bf16[512,1024]{1,0:T(8,128)(2,1)}), bf16[8192,1024]{1,0:T(8,128)(2,1)}) %all-gather.6.cloned.1.call-update) | async-done | bytes 16777232 | tf_op jit(solution)/shard_map/all_gather | solution.py:87
  315.2 0.2 mul.47
  315.5 14.8 %fusion.14 = (f32[1024]{0:T(1024)S(1)}, f32[512,1024]{1,0:T(8,128)S(1)}) fusion(f32[64,8,8,128]{3,2,1,0:T(8,128)S(1)} %bitcast.34, bf16[512,8192]{1,0:T(8,128)(2,1)} %all-gather.4.cloned.1.call-done, bf16[8192,1024]{1,0:T(8,128)(2,1)} %all-gather.6.cloned.1.call-done), kind=kOutput, calls=%fused_computation.43 | convolution fusion | flops 8591506432 | bytes 29364224 | tf_op jit(solution)/shard_map/dot_general | solution.py:85
  330.3 33.8 %psum.7 = f32[1024]{0:T(1024)S(1)} all-reduce(f32[1024]{0:T(1024)S(1)} %get-tuple-element.5), channel_id=1, replica_groups=mesh['row'=16,'col'=8] {'row'}, use_global_device_ids=true, to_apply=%region_4.5 | all-reduce | flops 1024 | bytes 8192 | tf_op jit(solution)/shard_map/psum | solution.py:91
  364.1 0.3 divide_bitcast_fusion
  364.4 0.5 copy.21
  364.9 1.9 fusion.5
  366.8 3.3 copy.12
  370.0 5.3 %all-to-all-start = ((f32[16,512,128]{2,1,0:T(8,128)}), f32[16,512,128]{2,1,0:T(8,128)}, u32[]{:S(2)}, u32[]{:S(2)}) async-start(f32[16,512,128]{2,1,0:T(8,128)} %copy.12), calls=%async_computation | async-start | bytes 8388608 | tf_op jit(solution)/shard_map/all_to_all | solution.py:93
  375.5 0.1 select_reduce_fusion.1
  375.6 0.4 select_reduce_fusion
  376.1 47.6 %all-to-all-done = f32[16,512,128]{2,1,0:T(8,128)} async-done(((f32[16,512,128]{2,1,0:T(8,128)}), f32[16,512,128]{2,1,0:T(8,128)}, u32[]{:S(2)}, u32[]{:S(2)}) %all-to-all-start) | async-done | bytes 4194336 | tf_op jit(solution)/shard_map/all_to_all | solution.py:93
  423.7 6.8 %fusion = f32[512,128,8]{1,2,0:T(8,128)S(1)} fusion(f32[8,16,1]{0,1,2:T(8,128)S(1)} %bitcast.35, f32[16,512,128]{2,1,0:T(8,128)} %all-to-all-done), kind=kOutput, calls=%fused_computation | convolution fusion | flops 100663296 | bytes 6291968 | tf_op jit(solution)/shard_map/sp,prb->rsb/dot_general | solution.py:54
  430.5 1.8 copy.33
  (18 shorter events, 0.4 us)
Async XLA Ops:
  6.5 196.6 %all-gather.4.cloned.1.call-start = ((), (), s32[]{:S(2)}) async-start(), calls=%async_computation.1 | async-start | bytes 9437184 | tf_op jit(solution)/shard_map/all_gather | solution.py:79
  6.5 1.6 copy-start
  36.8 0.8 copy-start.1
  36.8 278.4 %all-gather.6.cloned.1.call-start = ((), (), s32[]{:S(2)}) async-start(), calls=%async_computation.2 | async-start | bytes 17825792 | tf_op jit(solution)/shard_map/all_gather | solution.py:87
  370.0 53.7 %all-to-all-start = ((f32[16,512,128]{2,1,0:T(8,128)}), f32[16,512,128]{2,1,0:T(8,128)}, u32[]{:S(2)}, u32[]{:S(2)}) async-start(f32[16,512,128]{2,1,0:T(8,128)} %copy.12), calls=%async_computation | async-start | bytes 8388608 | tf_op jit(solution)/shard_map/all_to_all | solution.py:93
Sparse Core Ops, SparseCore 0:
  36.9 166.1 all-gather.3
  205.6 109.6 all-gather.5
